TPU v7x, 32 devices: a whole 2x2x4 slice. The times are simulated.
32 devices in a mesh: tm: 8 (over z, x), rows: 4 (over y, core).
Axes of the slice: x: 2, y: 2, z: 4, core: 2. Of those that a mesh axis runs over, the one named last changes fastest.
Arguments:
- latents: bfloat16 [32, 16, 32, 256], P('tm', 'rows'), may hold values from -6 to 6
- frame_gaps: float32 [32], P('tm'), may hold values from 0.5 to 250
- decay_rates: float32 [2, 256], replicated, may hold values from 0.0011 to 0.05
- input_kernel: bfloat16 [2, 3, 3, 256, 256], replicated, may hold values from -0.125 to 0.125
- output_kernel: bfloat16 [2, 3, 3, 256, 256], replicated, may hold values from -0.125 to 0.125
- feedthrough: float32 [2, 256], replicated, may hold values from -1 to 1
Outputs:
- encoded: bfloat16 [32, 16, 32, 256], P('tm', 'rows')
All inputs are finite; a program needn't handle non-finite values.
Results may differ from a plain program's by a relative error of at most 0.012.
Values may be sent and summed in bfloat16 or wider, within the bound.
A program may use at most 64 MiB of HBM per device.

v0:
```python
import jax
import jax.numpy as jnp
from jax import lax
from jax.sharding import PartitionSpec as P

STACK_COUNT = 2


def extended(cells, sides, width):
    for axis, dim in sides:
        count = lax.axis_size(axis)
        ends = count - 1
        head = lax.slice_in_dim(cells, 0, width, axis=dim)
        tail = lax.slice_in_dim(cells, cells.shape[dim] - width, cells.shape[dim], axis=dim)
        cells = jnp.concatenate(
            [
                lax.ppermute(tail, axis, [(i, (i + 1) % count) for i in range(ends)]),
                cells,
                lax.ppermute(head, axis, [((i + 1) % count, i) for i in range(ends)]),
            ],
            axis=dim,
        )
    return cells


def convolve(inputs, kernel):
    frames, vertical_extent, columns, channels = inputs.shape
    padded = extended(inputs, (("rows", 1),), 1)
    padded = jnp.pad(padded, ((0, 0), (0, 0), (1, 1), (0, 0)))
    summed = jnp.zeros((frames * vertical_extent * columns, kernel.shape[-1]), jnp.float32)
    for row_tap in range(3):
        for col_tap in range(3):
            window = padded[
                :, row_tap : row_tap + vertical_extent, col_tap : col_tap + columns, :
            ].reshape(-1, channels)
            summed = summed + jnp.dot(
                window, kernel[row_tap, col_tap], preferred_element_type=jnp.float32
            )
    return summed.reshape(frames, vertical_extent, columns, -1)


def local_states(driving, decays):

    def advance(carried, pieces):
        driven, factor = pieces
        carried = factor * carried + jnp.sqrt(1.0 - factor * factor) * driven
        return (carried, carried)

    initial = jnp.zeros(driving.shape[1:], jnp.float32)
    _, states = lax.scan(advance, initial, (driving, decays))
    return states


def combine(earlier, latter):
    return (earlier[0] * latter[0], latter[0] * earlier[1] + latter[1])


def carried_in(segment_attenuation, block_state):
    band, columns, channels = block_state.shape
    flat_state = block_state.reshape(1, band * columns, channels)
    flattened_decay = segment_attenuation.reshape(1, 1, channels)
    spread_decay, spread_state = (
        lax.all_to_all(flattened_decay, "tm", split_axis=2, concat_axis=0, tiled=True),
        lax.all_to_all(flat_state, "tm", split_axis=2, concat_axis=0, tiled=True),
    )
    _, inclusive = lax.associative_scan(combine, (spread_decay, spread_state), axis=0)
    exclusive = jnp.concatenate([jnp.zeros_like(inclusive[:1]), inclusive[:-1]], axis=0)
    returned = lax.all_to_all(
        exclusive.astype(jnp.bfloat16), "tm", split_axis=0, concat_axis=2, tiled=True
    ).astype(exclusive.dtype)
    incoming = returned.reshape(band, columns, channels)
    return incoming


def per_device(latents, frame_gaps, decay_rates, input_kernel, output_kernel, feedthrough):
    inputs = latents
    for layer_index in range(STACK_COUNT):
        layer_rates = decay_rates[layer_index]
        decays = jnp.exp(-frame_gaps[:, None] * layer_rates[None, :])
        driving = convolve(inputs, input_kernel[layer_index])
        states = local_states(driving, decays)
        cumulative = jnp.cumprod(decays, axis=0)
        incoming = carried_in(cumulative[-1], states[-1])
        states = states + cumulative[:, None, None, :] * incoming[None]
        rounded_states = states.astype(jnp.bfloat16)
        premix = convolve(rounded_states, output_kernel[layer_index]) + feedthrough[
            layer_index
        ] * inputs.astype(jnp.float32)
        inputs = jax.nn.gelu(premix, approximate=True).astype(jnp.bfloat16)
    return inputs


def solution(mesh):
    in_specs = (P("tm", "rows", None, None), P("tm"), P(), P(), P(), P())
    out_specs = P("tm", "rows", None, None)
    return jax.shard_map(
        per_device, mesh=mesh, in_specs=in_specs, out_specs=out_specs, check_vma=False
    )
```

profile of v0, /device:TPU:1, one launch (start us, length us, event | category | flops | bytes accessed | tf_op | source)
XLA Modules:
  0.0 124.7 jit_solution(17457823050170934931)
XLA Ops:
  0.0 0.9 fusion.48
  0.9 4.5 %collective-permute-start = (bf16[4,1,32,256]{3,2,1,0:T(8,128)(2,1)S(1)}, bf16[4,1,32,256]{3,2,1,0:T(8,128)(2,1)S(1)}, u32[]{:S(2)}, u32[]{:S(2)}) collective-permute-start(bf16[4,1,32,256]{3,2,1,0:T(8,128)(2,1)S(1)} %get-tuple-element.163), channel_id=1, source_target_pairs={{0,1},{1,2},{2,3},{4,5},{5,6},{6,7},{8,9},{9,10},{10,11},{12,13},{... | collective-permute-start | bytes 196616 | tf_op jit(solution)/shard_map/ppermute | solution.py:17
  5.4 1.9 %collective-permute-start.1 = (bf16[4,1,32,256]{3,2,1,0:T(8,128)(2,1)S(1)}, bf16[4,1,32,256]{3,2,1,0:T(8,128)(2,1)S(1)}, u32[]{:S(2)}, u32[]{:S(2)}) collective-permute-start(bf16[4,1,32,256]{3,2,1,0:T(8,128)(2,1)S(1)} %get-tuple-element.164), channel_id=1, source_target_pairs={{1,0},{2,1},{3,2},{5,4},{6,5},{7,6},{9,8},{10,9},{11,10},{13,12},{... | collective-permute-start | bytes 196616 | tf_op jit(solution)/shard_map/ppermute | solution.py:19
  7.3 0.8 fusion.52
  8.1 0.7 neg.5
  8.9 0.8 copy.39
  9.7 5.5 %all-to-all-start.1 = ((f32[1,1,256]{1,0,2:T(1,128)}), f32[1,1,256]{1,0,2:T(1,128)S(1)}, u32[]{:S(2)}, u32[]{:S(2)}) async-start(f32[1,1,256]{1,0,2:T(1,128)} %copy.39), calls=%async_computation.1 | async-start | bytes 262144 | tf_op jit(solution)/shard_map/all_to_all | solution.py:63
  15.2 1.8 %slice_bitcast_fusion.1 = (bf16[3,3,256,256]{3,2,1,0:T(8,128)(2,1)S(1)}, bf16[3,3,256,256]{3,2,1,0:T(8,128)(2,1)S(1)}) fusion(bf16[2,3,3,256,256]{4,3,2,1,0:T(8,128)(2,1)} %param.13), kind=kLoop, calls=%fused_computation.47 | loop fusion | bytes 4718592 | tf_op jit(solution)/shard_map/squeeze | solution.py:80
  17.1 4.4 %all-to-all-done.1 = f32[1,1,256]{1,0,2:T(1,128)S(1)} async-done(((f32[1,1,256]{1,0,2:T(1,128)}), f32[1,1,256]{1,0,2:T(1,128)S(1)}, u32[]{:S(2)}, u32[]{:S(2)}) %all-to-all-start.1) | async-done | bytes 1056 | tf_op jit(solution)/shard_map/all_to_all | solution.py:63
  21.4 1.0 reduce
  22.7 0.2 select_maximum_fusion.6
  22.9 0.3 fusion.44
  23.4 0.2 fusion.29
  24.6 0.2 convolution_add_fusion.23
  25.1 1.0 fusion.5
  26.2 4.1 %while.26 = (s32[]{:T(128)}, f32[4,32,256]{2,1,0:T(8,128)S(1)}, f32[4,4,32,256]{3,2,1,0:T(8,128)S(1)}, f32[4,256]{1,0:T(4,128)S(1)}, f32[4,4,32,256]{3,2,1,0:T(8,128)}, /*index=5*/s32[]{:T(128)}, s32[]{:T(128)}) while((s32[]{:T(128)}, f32[4,32,256]{2,1,0:T(8,128)S(1)}, f32[4,4,32,256]{3,2,1,0:T(8,128)S(1)}, ...), condition=%wide.region_1.2_spmd.clone, body=%wide.region_0.1_spmd.clone.sunk | while | flops 131587 | bytes 530527 | solution.py:50
  26.2 1.0 bitcast_dynamic-update-slice_fusion.4
  27.2 1.0 bitcast_dynamic-update-slice_fusion.4
  28.3 1.0 bitcast_dynamic-update-slice_fusion.4
  29.3 1.0 bitcast_dynamic-update-slice_fusion.4
  30.3 0.8 copy.37
  31.0 3.4 %all-to-all-start = ((f32[1,128,256]{1,0,2:T(1,128)}), f32[1,128,256]{1,0,2:T(1,128)S(1)}, u32[]{:S(2)}, u32[]{:S(2)}) async-start(f32[1,128,256]{1,0,2:T(1,128)} %copy.37), calls=%async_computation | async-start | bytes 262144 | tf_op jit(solution)/shard_map/all_to_all | solution.py:64
  34.5 7.2 %all-to-all-done = f32[1,128,256]{1,0,2:T(1,128)S(1)} async-done(((f32[1,128,256]{1,0,2:T(1,128)}), f32[1,128,256]{1,0,2:T(1,128)S(1)}, u32[]{:S(2)}, u32[]{:S(2)}) %all-to-all-start) | async-done | bytes 131104 | tf_op jit(solution)/shard_map/all_to_all | solution.py:64
  42.3 0.6 concatenate.59
  42.9 3.4 %all-to-all-start.2 = ((bf16[8,128,32]{1,2,0:T(8,128)(2,1)}), bf16[8,128,32]{1,2,0:T(8,128)(2,1)S(1)}, u32[]{:S(2)}, u32[]{:S(2)}) async-start(bf16[8,128,32]{1,2,0:T(8,128)(2,1)} %concatenate.59), calls=%async_computation.2 | async-start | bytes 131072 | tf_op jit(solution)/shard_map/all_to_all | solution.py:68
  46.3 2.8 %slice_bitcast_fusion = (bf16[3,3,256,256]{3,2,1,0:T(8,128)(2,1)S(1)}, bf16[3,3,256,256]{3,2,1,0:T(8,128)(2,1)}) fusion(bf16[2,3,3,256,256]{4,3,2,1,0:T(8,128)(2,1)} %param.14), kind=kLoop, calls=%fused_computation.46 | loop fusion | bytes 4718592 | tf_op jit(solution)/shard_map/squeeze | solution.py:86
  49.2 2.8 %all-to-all-done.2 = bf16[8,128,32]{1,2,0:T(8,128)(2,1)S(1)} async-done(((bf16[8,128,32]{1,2,0:T(8,128)(2,1)}), bf16[8,128,32]{1,2,0:T(8,128)(2,1)S(1)}, u32[]{:S(2)}, u32[]{:S(2)}) %all-to-all-start.2) | async-done | bytes 65568 | tf_op jit(solution)/shard_map/all_to_all | solution.py:68
  52.0 1.1 reshape.228
  53.1 1.2 copy.45
  54.4 6.2 %collective-permute-start.2 = (bf16[4,1,32,256]{3,2,1,0:T(8,128)(2,1)S(1)}, bf16[4,1,32,256]{3,2,1,0:T(8,128)(2,1)S(1)}, u32[]{:S(2)}, u32[]{:S(2)}) collective-permute-start(bf16[4,1,32,256]{3,2,1,0:T(8,128)(2,1)S(1)} %get-tuple-element.159), channel_id=1, source_target_pairs={{0,1},{1,2},{2,3},{4,5},{5,6},{6,7},{8,9},{9,10},{10,11},{12,13},{... | collective-permute-start | bytes 196616 | tf_op jit(solution)/shard_map/ppermute | solution.py:17
  60.7 1.9 %collective-permute-start.3 = (bf16[4,1,32,256]{3,2,1,0:T(8,128)(2,1)S(1)}, bf16[4,1,32,256]{3,2,1,0:T(8,128)(2,1)S(1)}, u32[]{:S(2)}, u32[]{:S(2)}) collective-permute-start(bf16[4,1,32,256]{3,2,1,0:T(8,128)(2,1)S(1)} %get-tuple-element.160), channel_id=1, source_target_pairs={{1,0},{2,1},{3,2},{5,4},{6,5},{7,6},{9,8},{10,9},{11,10},{13,12},{... | collective-permute-start | bytes 196616 | tf_op jit(solution)/shard_map/ppermute | solution.py:19
  62.7 3.6 %collective-permute-done.3 = bf16[4,1,32,256]{3,2,1,0:T(8,128)(2,1)S(1)} collective-permute-done((bf16[4,1,32,256]{3,2,1,0:T(8,128)(2,1)S(1)}, bf16[4,1,32,256]{3,2,1,0:T(8,128)(2,1)S(1)}, u32[]{:S(2)}, u32[]{:S(2)}) %collective-permute-start.3) | collective-permute-done | bytes 65568 | tf_op jit(solution)/shard_map/ppermute | solution.py:19
  66.2 0.2 select_maximum_fusion.4
  66.5 0.3 fusion.43
  66.8 1.0 copy-done.1
  68.9 0.2 convolution_add_fusion.17
  69.6 0.2 fusion.4
  69.9 0.2 fusion.14
  70.1 1.9 %collective-permute-start.4 = (bf16[4,1,32,256]{3,2,1,0:T(8,128)(2,1)S(1)}, bf16[4,1,32,256]{3,2,1,0:T(8,128)(2,1)S(1)}, u32[]{:S(2)}, u32[]{:S(2)}) collective-permute-start(bf16[4,1,32,256]{3,2,1,0:T(8,128)(2,1)S(1)} %get-tuple-element.155), channel_id=1, source_target_pairs={{0,1},{1,2},{2,3},{4,5},{5,6},{6,7},{8,9},{9,10},{10,11},{12,13},{... | collective-permute-start | bytes 196616 | tf_op jit(solution)/shard_map/ppermute | solution.py:17
  72.0 2.4 %collective-permute-start.5 = (bf16[4,1,32,256]{3,2,1,0:T(8,128)(2,1)S(1)}, bf16[4,1,32,256]{3,2,1,0:T(8,128)(2,1)S(1)}, u32[]{:S(2)}, u32[]{:S(2)}) collective-permute-start(bf16[4,1,32,256]{3,2,1,0:T(8,128)(2,1)S(1)} %get-tuple-element.156), channel_id=1, source_target_pairs={{1,0},{2,1},{3,2},{5,4},{6,5},{7,6},{9,8},{10,9},{11,10},{13,12},{... | collective-permute-start | bytes 196616 | tf_op jit(solution)/shard_map/ppermute | solution.py:19
  74.5 0.8 copy.43
  75.3 3.4 %all-to-all-start.4 = ((f32[1,1,256]{1,0,2:T(1,128)}), f32[1,1,256]{1,0,2:T(1,128)S(1)}, u32[]{:S(2)}, u32[]{:S(2)}) async-start(f32[1,1,256]{1,0,2:T(1,128)} %copy.43), calls=%async_computation.4 | async-start | bytes 262144 | tf_op jit(solution)/shard_map/all_to_all | solution.py:63
  78.7 7.0 %all-to-all-done.4 = f32[1,1,256]{1,0,2:T(1,128)S(1)} async-done(((f32[1,1,256]{1,0,2:T(1,128)}), f32[1,1,256]{1,0,2:T(1,128)S(1)}, u32[]{:S(2)}, u32[]{:S(2)}) %all-to-all-start.4) | async-done | bytes 1056 | tf_op jit(solution)/shard_map/all_to_all | solution.py:63
  85.7 1.0 reduce.1
  86.9 0.2 select_maximum_fusion.2
  87.1 0.3 fusion.42
  87.4 0.2 fusion.26
  89.3 0.2 fusion.3
  89.6 0.5 while.27
  90.2 0.8 copy.41
  90.9 3.4 %all-to-all-start.3 = ((f32[1,128,256]{1,0,2:T(1,128)}), f32[1,128,256]{1,0,2:T(1,128)S(1)}, u32[]{:S(2)}, u32[]{:S(2)}) async-start(f32[1,128,256]{1,0,2:T(1,128)} %copy.41), calls=%async_computation.3 | async-start | bytes 262144 | tf_op jit(solution)/shard_map/all_to_all | solution.py:64
  94.4 6.1 %all-to-all-done.3 = f32[1,128,256]{1,0,2:T(1,128)S(1)} async-done(((f32[1,128,256]{1,0,2:T(1,128)}), f32[1,128,256]{1,0,2:T(1,128)S(1)}, u32[]{:S(2)}, u32[]{:S(2)}) %all-to-all-start.3) | async-done | bytes 131104 | tf_op jit(solution)/shard_map/all_to_all | solution.py:64
  101.1 8.9 %all_to_all.78 = bf16[8,128,32]{1,2,0:T(8,128)(2,1)S(1)} all-to-all(bf16[8,128,32]{1,2,0:T(8,128)(2,1)S(1)} %concatenate.68), channel_id=1, replica_groups=mesh['tm'=8,'rows'=4] {'tm'}, dimensions={0} | all-to-all | bytes 131072 | tf_op jit(solution)/shard_map/all_to_all | solution.py:68
  110.1 0.3 reshape.229
  110.6 4.9 %collective-permute-start.6 = (bf16[4,1,32,256]{3,2,1,0:T(8,128)(2,1)S(1)}, bf16[4,1,32,256]{3,2,1,0:T(8,128)(2,1)S(1)}, u32[]{:S(2)}, u32[]{:S(2)}) collective-permute-start(bf16[4,1,32,256]{3,2,1,0:T(8,128)(2,1)S(1)} %get-tuple-element.151), channel_id=1, source_target_pairs={{0,1},{1,2},{2,3},{4,5},{5,6},{6,7},{8,9},{9,10},{10,11},{12,13},{... | collective-permute-start | bytes 196616 | tf_op jit(solution)/shard_map/ppermute | solution.py:17
  115.5 1.9 %collective-permute-start.7 = (bf16[4,1,32,256]{3,2,1,0:T(8,128)(2,1)S(1)}, bf16[4,1,32,256]{3,2,1,0:T(8,128)(2,1)S(1)}, u32[]{:S(2)}, u32[]{:S(2)}) collective-permute-start(bf16[4,1,32,256]{3,2,1,0:T(8,128)(2,1)S(1)} %get-tuple-element.152), channel_id=1, source_target_pairs={{1,0},{2,1},{3,2},{5,4},{6,5},{7,6},{9,8},{10,9},{11,10},{13,12},{... | collective-permute-start | bytes 196616 | tf_op jit(solution)/shard_map/ppermute | solution.py:19
  117.5 3.6 %collective-permute-done.7 = bf16[4,1,32,256]{3,2,1,0:T(8,128)(2,1)S(1)} collective-permute-done((bf16[4,1,32,256]{3,2,1,0:T(8,128)(2,1)S(1)}, bf16[4,1,32,256]{3,2,1,0:T(8,128)(2,1)S(1)}, u32[]{:S(2)}, u32[]{:S(2)}) %collective-permute-start.7) | collective-permute-done | bytes 65568 | tf_op jit(solution)/shard_map/ppermute | solution.py:19
  121.1 0.2 select_maximum_fusion
  121.3 0.3 fusion.41
  121.6 0.2 fusion.24
  122.1 0.2 convolution_add_fusion.6
  122.4 0.2 convolution_add_fusion.5
  123.5 0.2 fusion.2
  123.8 0.9 fusion.22
  (131 shorter events, 8.4 us)
Async XLA Ops:
  0.9 21.8 %collective-permute-start = (bf16[4,1,32,256]{3,2,1,0:T(8,128)(2,1)S(1)}, bf16[4,1,32,256]{3,2,1,0:T(8,128)(2,1)S(1)}, u32[]{:S(2)}, u32[]{:S(2)}) collective-permute-start(bf16[4,1,32,256]{3,2,1,0:T(8,128)(2,1)S(1)} %get-tuple-element.163), channel_id=1, source_target_pairs={{0,1},{1,2},{2,3},{4,5},{5,6},{6,7},{8,9},{9,10},{10,11},{12,13},{... | collective-permute-start | bytes 196616 | tf_op jit(solution)/shard_map/ppermute | solution.py:17
  5.4 17.2 %collective-permute-start.1 = (bf16[4,1,32,256]{3,2,1,0:T(8,128)(2,1)S(1)}, bf16[4,1,32,256]{3,2,1,0:T(8,128)(2,1)S(1)}, u32[]{:S(2)}, u32[]{:S(2)}) collective-permute-start(bf16[4,1,32,256]{3,2,1,0:T(8,128)(2,1)S(1)} %get-tuple-element.164), channel_id=1, source_target_pairs={{1,0},{2,1},{3,2},{5,4},{6,5},{7,6},{9,8},{10,9},{11,10},{13,12},{... | collective-permute-start | bytes 196616 | tf_op jit(solution)/shard_map/ppermute | solution.py:19
  9.7 11.7 %all-to-all-start.1 = ((f32[1,1,256]{1,0,2:T(1,128)}), f32[1,1,256]{1,0,2:T(1,128)S(1)}, u32[]{:S(2)}, u32[]{:S(2)}) async-start(f32[1,1,256]{1,0,2:T(1,128)} %copy.39), calls=%async_computation.1 | async-start | bytes 262144 | tf_op jit(solution)/shard_map/all_to_all | solution.py:63
  15.2 7.4 %copy-start = (bf16[4,4,32,256]{3,2,1,0:T(8,128)(2,1)S(1)}, bf16[4,4,32,256]{3,2,1,0:T(8,128)(2,1)}, u32[]{:S(2)}) copy-start(bf16[4,4,32,256]{3,2,1,0:T(8,128)(2,1)} %param.10) | copy-start | bytes 786436
  31.0 10.6 %all-to-all-start = ((f32[1,128,256]{1,0,2:T(1,128)}), f32[1,128,256]{1,0,2:T(1,128)S(1)}, u32[]{:S(2)}, u32[]{:S(2)}) async-start(f32[1,128,256]{1,0,2:T(1,128)} %copy.37), calls=%async_computation | async-start | bytes 262144 | tf_op jit(solution)/shard_map/all_to_all | solution.py:64
  42.9 9.1 %all-to-all-start.2 = ((bf16[8,128,32]{1,2,0:T(8,128)(2,1)}), bf16[8,128,32]{1,2,0:T(8,128)(2,1)S(1)}, u32[]{:S(2)}, u32[]{:S(2)}) async-start(bf16[8,128,32]{1,2,0:T(8,128)(2,1)} %concatenate.59), calls=%async_computation.2 | async-start | bytes 131072 | tf_op jit(solution)/shard_map/all_to_all | solution.py:68
  52.0 10.6 %copy-start.2 = (f32[2,256]{1,0:T(2,128)S(1)}, f32[2,256]{1,0:T(2,128)}, u32[]{:S(2)}) copy-start(f32[2,256]{1,0:T(2,128)} %param.15) | copy-start | bytes 6148
  54.4 8.2 %collective-permute-start.2 = (bf16[4,1,32,256]{3,2,1,0:T(8,128)(2,1)S(1)}, bf16[4,1,32,256]{3,2,1,0:T(8,128)(2,1)S(1)}, u32[]{:S(2)}, u32[]{:S(2)}) collective-permute-start(bf16[4,1,32,256]{3,2,1,0:T(8,128)(2,1)S(1)} %get-tuple-element.159), channel_id=1, source_target_pairs={{0,1},{1,2},{2,3},{4,5},{5,6},{6,7},{8,9},{9,10},{10,11},{12,13},{... | collective-permute-start | bytes 196616 | tf_op jit(solution)/shard_map/ppermute | solution.py:17
  60.7 5.6 %collective-permute-start.3 = (bf16[4,1,32,256]{3,2,1,0:T(8,128)(2,1)S(1)}, bf16[4,1,32,256]{3,2,1,0:T(8,128)(2,1)S(1)}, u32[]{:S(2)}, u32[]{:S(2)}) collective-permute-start(bf16[4,1,32,256]{3,2,1,0:T(8,128)(2,1)S(1)} %get-tuple-element.160), channel_id=1, source_target_pairs={{1,0},{2,1},{3,2},{5,4},{6,5},{7,6},{9,8},{10,9},{11,10},{13,12},{... | collective-permute-start | bytes 196616 | tf_op jit(solution)/shard_map/ppermute | solution.py:19
  66.5 1.3 %copy-start.1 = (bf16[3,3,256,256]{3,2,1,0:T(8,128)(2,1)S(1)}, bf16[3,3,256,256]{3,2,1,0:T(8,128)(2,1)}, u32[]{:S(2)}) copy-start(bf16[3,3,256,256]{3,2,1,0:T(8,128)(2,1)} %get-tuple-element.122) | copy-start | bytes 3538948
  70.1 16.8 %collective-permute-start.4 = (bf16[4,1,32,256]{3,2,1,0:T(8,128)(2,1)S(1)}, bf16[4,1,32,256]{3,2,1,0:T(8,128)(2,1)S(1)}, u32[]{:S(2)}, u32[]{:S(2)}) collective-permute-start(bf16[4,1,32,256]{3,2,1,0:T(8,128)(2,1)S(1)} %get-tuple-element.155), channel_id=1, source_target_pairs={{0,1},{1,2},{2,3},{4,5},{5,6},{6,7},{8,9},{9,10},{10,11},{12,13},{... | collective-permute-start | bytes 196616 | tf_op jit(solution)/shard_map/ppermute | solution.py:17
  72.0 14.8 %collective-permute-start.5 = (bf16[4,1,32,256]{3,2,1,0:T(8,128)(2,1)S(1)}, bf16[4,1,32,256]{3,2,1,0:T(8,128)(2,1)S(1)}, u32[]{:S(2)}, u32[]{:S(2)}) collective-permute-start(bf16[4,1,32,256]{3,2,1,0:T(8,128)(2,1)S(1)} %get-tuple-element.156), channel_id=1, source_target_pairs={{1,0},{2,1},{3,2},{5,4},{6,5},{7,6},{9,8},{10,9},{11,10},{13,12},{... | collective-permute-start | bytes 196616 | tf_op jit(solution)/shard_map/ppermute | solution.py:19
  75.3 10.4 %all-to-all-start.4 = ((f32[1,1,256]{1,0,2:T(1,128)}), f32[1,1,256]{1,0,2:T(1,128)S(1)}, u32[]{:S(2)}, u32[]{:S(2)}) async-start(f32[1,1,256]{1,0,2:T(1,128)} %copy.43), calls=%async_computation.4 | async-start | bytes 262144 | tf_op jit(solution)/shard_map/all_to_all | solution.py:63
  90.9 9.6 %all-to-all-start.3 = ((f32[1,128,256]{1,0,2:T(1,128)}), f32[1,128,256]{1,0,2:T(1,128)S(1)}, u32[]{:S(2)}, u32[]{:S(2)}) async-start(f32[1,128,256]{1,0,2:T(1,128)} %copy.41), calls=%async_computation.3 | async-start | bytes 262144 | tf_op jit(solution)/shard_map/all_to_all | solution.py:64
  110.6 6.8 %collective-permute-start.6 = (bf16[4,1,32,256]{3,2,1,0:T(8,128)(2,1)S(1)}, bf16[4,1,32,256]{3,2,1,0:T(8,128)(2,1)S(1)}, u32[]{:S(2)}, u32[]{:S(2)}) collective-permute-start(bf16[4,1,32,256]{3,2,1,0:T(8,128)(2,1)S(1)} %get-tuple-element.151), channel_id=1, source_target_pairs={{0,1},{1,2},{2,3},{4,5},{5,6},{6,7},{8,9},{9,10},{10,11},{12,13},{... | collective-permute-start | bytes 196616 | tf_op jit(solution)/shard_map/ppermute | solution.py:17
  115.5 5.6 %collective-permute-start.7 = (bf16[4,1,32,256]{3,2,1,0:T(8,128)(2,1)S(1)}, bf16[4,1,32,256]{3,2,1,0:T(8,128)(2,1)S(1)}, u32[]{:S(2)}, u32[]{:S(2)}) collective-permute-start(bf16[4,1,32,256]{3,2,1,0:T(8,128)(2,1)S(1)} %get-tuple-element.152), channel_id=1, source_target_pairs={{1,0},{2,1},{3,2},{5,4},{6,5},{7,6},{9,8},{10,9},{11,10},{13,12},{... | collective-permute-start | bytes 196616 | tf_op jit(solution)/shard_map/ppermute | solution.py:19
where the time goes:
time: 126 us; the launch traced here: 125 us
  starting transfers between devices  44.8 us (36%)
  waiting for transfers between devices  34.8 us (28%)
  local copies, waits for them, and re-layouts  15.8 us (13%)
  other arithmetic  10.4 us (8%)
  blocking collectives  8.91 us (7%)
  matrix products  8.88 us (7%)
    ppermute x4, starting transfers between devices, extended(): lax.ppermute(tail, axis, [(i, (i + 1) % count) for i in range(ends)])  17.6 us
    all_to_all x2, waiting for transfers between devices, carried_in(): lax.all_to_all(flat_state, 'tm', split_axis=2, concat_axis=0, tiled=True)  13.4 us
    all_to_all x2, waiting for transfers between devices, carried_in(): lax.all_to_all(flattened_decay, 'tm', split_axis=2, concat_axis=0, tiled=...  11.3 us
    all_to_all x1, blocking collectives, carried_in(): lax.all_to_all(exclusive.astype(jnp.bfloat16), 'tm', split_axis=0, concat...  8.91 us
    all_to_all x2, starting transfers between devices, carried_in(): lax.all_to_all(flattened_decay, 'tm', split_axis=2, concat_axis=0, tiled=...  8.9 us
    dot_general x36, matrix products, convolve(): jnp.dot(window, kernel[row_tap, col_tap], preferred_element_type=jnp.floa...  8.88 us
    ppermute x4, starting transfers between devices, extended(): lax.ppermute(head, axis, [((i + 1) % count, i) for i in range(ends)])  8.17 us
    ppermute x4, waiting for transfers between devices, extended(): lax.ppermute(head, axis, [((i + 1) % count, i) for i in range(ends)])  7.24 us
  transfers between devices with their start and end apart: 13, of which 7 were waited for; matrix products, arithmetic and copies ran while one was open for 8% of the time, Pallas kernels for 0%

commit v1 on v0

--- a/solution.py
+++ b/solution.py
@@ -4,6 +4,13 @@
 from jax.sharding import PartitionSpec as P
 
 STACK_COUNT = 2
+
+
+def stacked_exchange(shard, name, split, join):
+    peers = lax.axis_size(name)
+    tiles = jnp.stack(jnp.split(shard, peers, axis=split), axis=0)
+    tiles = lax.all_to_all(tiles, name, split_axis=0, concat_axis=0)
+    return jnp.concatenate(tiles, axis=join)
 
 
 def extended(cells, sides, width):
@@ -61,7 +68,7 @@
     flattened_decay = segment_attenuation.reshape(1, 1, channels)
     spread_decay, spread_state = (
         lax.all_to_all(flattened_decay, "tm", split_axis=2, concat_axis=0, tiled=True),
-        lax.all_to_all(flat_state, "tm", split_axis=2, concat_axis=0, tiled=True),
+        stacked_exchange(flat_state, "tm", 2, 0),
     )
     _, inclusive = lax.associative_scan(combine, (spread_decay, spread_state), axis=0)
     exclusive = jnp.concatenate([jnp.zeros_like(inclusive[:1]), inclusive[:-1]], axis=0)

time: 126 us -> 136 us (1.079)
  local copies, waits for them, and re-layouts: 15.8 us -> 25.6 us
    unnamed x8 -> x22, local copies, waits for them, and re-layouts: 1.05 us -> 9.65 us
    another operation x4 -> x22, local copies, waits for them, and re-layouts: 1.6 us -> 2.73 us  [the longest x20 2.65 us: stacked_exchange(): tiles = jnp.stack(jnp.split(shard, peers, axis=split), axis=0)]
where the time goes in v1:
time: 136 us; the launch traced here: 135 us
  starting transfers between devices  44.8 us (33%)
  waiting for transfers between devices  34.8 us (26%)
  local copies, waits for them, and re-layouts  25.6 us (19%)
  other arithmetic  10.4 us (8%)
  blocking collectives  8.92 us (7%)
  matrix products  8.89 us (7%)
    ppermute x4, starting transfers between devices, extended(): lax.ppermute(tail, axis, [(i, (i + 1) % count) for i in range(ends)])  17.6 us
    all_to_all x2, waiting for transfers between devices, stacked_exchange(): tiles = lax.all_to_all(tiles, name, split_axis=0, concat_axis=0)  13.4 us
    all_to_all x2, waiting for transfers between devices, carried_in(): lax.all_to_all(flattened_decay, 'tm', split_axis=2, concat_axis=0, tiled=...  11.3 us
    unnamed x22, local copies, waits for them, and re-layouts  9.65 us
    all_to_all x1, blocking collectives, carried_in(): lax.all_to_all(exclusive.astype(jnp.bfloat16), 'tm', split_axis=0, concat...  8.92 us
    all_to_all x2, starting transfers between devices, carried_in(): lax.all_to_all(flattened_decay, 'tm', split_axis=2, concat_axis=0, tiled=...  8.9 us
    dot_general x36, matrix products, convolve(): jnp.dot(window, kernel[row_tap, col_tap], preferred_element_type=jnp.floa...  8.89 us
    ppermute x4, starting transfers between devices, extended(): lax.ppermute(head, axis, [((i + 1) % count, i) for i in range(ends)])  8.17 us
  transfers between devices with their start and end apart: 13, of which 7 were waited for; matrix products, arithmetic and copies ran while one was open for 8% of the time, Pallas kernels for 0%

profile of v1, /device:TPU:1, one launch (start us, length us, event | category | flops | bytes accessed | tf_op | source)
XLA Modules:
  0.0 134.5 jit_solution(10853857078694607525)
XLA Ops:
  0.0 0.9 fusion.48
  0.9 4.5 %collective-permute-start = (bf16[4,1,32,256]{3,2,1,0:T(8,128)(2,1)S(1)}, bf16[4,1,32,256]{3,2,1,0:T(8,128)(2,1)S(1)}, u32[]{:S(2)}, u32[]{:S(2)}) collective-permute-start(bf16[4,1,32,256]{3,2,1,0:T(8,128)(2,1)S(1)} %get-tuple-element.163), channel_id=1, source_target_pairs={{0,1},{1,2},{2,3},{4,5},{5,6},{6,7},{8,9},{9,10},{10,11},{12,13},{... | collective-permute-start | bytes 196616 | tf_op jit(solution)/shard_map/ppermute | solution.py:24
  5.4 1.9 %collective-permute-start.1 = (bf16[4,1,32,256]{3,2,1,0:T(8,128)(2,1)S(1)}, bf16[4,1,32,256]{3,2,1,0:T(8,128)(2,1)S(1)}, u32[]{:S(2)}, u32[]{:S(2)}) collective-permute-start(bf16[4,1,32,256]{3,2,1,0:T(8,128)(2,1)S(1)} %get-tuple-element.164), channel_id=1, source_target_pairs={{1,0},{2,1},{3,2},{5,4},{6,5},{7,6},{9,8},{10,9},{11,10},{13,12},{... | collective-permute-start | bytes 196616 | tf_op jit(solution)/shard_map/ppermute | solution.py:26
  7.3 0.8 fusion.52
  8.1 0.7 neg.5
  8.9 0.8 copy.31
  9.7 5.5 %all-to-all-start.1 = ((f32[1,1,256]{1,0,2:T(1,128)}), f32[1,1,256]{1,0,2:T(1,128)S(1)}, u32[]{:S(2)}, u32[]{:S(2)}) async-start(f32[1,1,256]{1,0,2:T(1,128)} %copy.31), calls=%async_computation.1 | async-start | bytes 262144 | tf_op jit(solution)/shard_map/all_to_all | solution.py:70
  15.2 1.9 %slice_bitcast_fusion.1 = (bf16[3,3,256,256]{3,2,1,0:T(8,128)(2,1)S(1)}, bf16[3,3,256,256]{3,2,1,0:T(8,128)(2,1)S(1)}) fusion(bf16[2,3,3,256,256]{4,3,2,1,0:T(8,128)(2,1)} %param.13), kind=kLoop, calls=%fused_computation.47 | loop fusion | bytes 4718592 | tf_op jit(solution)/shard_map/squeeze | solution.py:87
  17.1 4.3 %all-to-all-done.1 = f32[1,1,256]{1,0,2:T(1,128)S(1)} async-done(((f32[1,1,256]{1,0,2:T(1,128)}), f32[1,1,256]{1,0,2:T(1,128)S(1)}, u32[]{:S(2)}, u32[]{:S(2)}) %all-to-all-start.1) | async-done | bytes 1056 | tf_op jit(solution)/shard_map/all_to_all | solution.py:70
  21.4 1.0 reduce
  22.9 0.3 fusion.44
  25.1 1.0 fusion.5
  26.2 4.1 %while.26 = (s32[]{:T(128)}, f32[4,32,256]{2,1,0:T(8,128)S(1)}, f32[4,4,32,256]{3,2,1,0:T(8,128)S(1)}, f32[4,256]{1,0:T(4,128)S(1)}, f32[4,4,32,256]{3,2,1,0:T(8,128)}, /*index=5*/s32[]{:T(128)}, s32[]{:T(128)}) while((s32[]{:T(128)}, f32[4,32,256]{2,1,0:T(8,128)S(1)}, f32[4,4,32,256]{3,2,1,0:T(8,128)S(1)}, ...), condition=%wide.region_1.2_spmd.clone, body=%wide.region_0.1_spmd.clone.sunk | while | flops 131587 | bytes 530527 | solution.py:57
  26.2 1.0 bitcast_dynamic-update-slice_fusion.4
  27.2 1.0 bitcast_dynamic-update-slice_fusion.4
  28.3 1.0 bitcast_dynamic-update-slice_fusion.4
  29.3 1.0 bitcast_dynamic-update-slice_fusion.4
  30.5 0.6 constant_dynamic-update-slice_fusion.7
  31.6 0.6 constant_dynamic-update-slice_fusion.6
  32.3 0.6 constant_dynamic-update-slice_fusion.5
  32.9 0.6 constant_dynamic-update-slice_fusion.4
  33.5 0.6 constant_dynamic-update-slice_fusion.3
  34.1 0.6 constant_dynamic-update-slice_fusion.2
  34.7 0.6 constant_dynamic-update-slice_fusion.1
  35.3 0.6 constant_dynamic-update-slice_fusion
  35.9 3.4 %all-to-all-start = ((f32[8,1,128,32]{2,3,1,0:T(8,128)}), f32[8,1,128,32]{2,3,1,0:T(8,128)S(1)}, u32[]{:S(2)}, u32[]{:S(2)}) async-start(f32[8,1,128,32]{2,3,1,0:T(8,128)} %constant_dynamic-update-slice_fusion), calls=%async_computation | async-start | bytes 262144 | tf_op jit(solution)/shard_map/all_to_all | solution.py:12
  39.3 7.2 %all-to-all-done = f32[8,1,128,32]{2,3,1,0:T(8,128)S(1)} async-done(((f32[8,1,128,32]{2,3,1,0:T(8,128)}), f32[8,1,128,32]{2,3,1,0:T(8,128)S(1)}, u32[]{:S(2)}, u32[]{:S(2)}) %all-to-all-start) | async-done | bytes 131104 | tf_op jit(solution)/shard_map/all_to_all | solution.py:12
  47.2 0.6 concatenate.59
  47.8 3.4 %all-to-all-start.2 = ((bf16[8,128,32]{1,2,0:T(8,128)(2,1)}), bf16[8,128,32]{1,2,0:T(8,128)(2,1)S(1)}, u32[]{:S(2)}, u32[]{:S(2)}) async-start(bf16[8,128,32]{1,2,0:T(8,128)(2,1)} %concatenate.59), calls=%async_computation.2 | async-start | bytes 131072 | tf_op jit(solution)/shard_map/all_to_all | solution.py:75
  51.2 2.9 %slice_bitcast_fusion = (bf16[3,3,256,256]{3,2,1,0:T(8,128)(2,1)S(1)}, bf16[3,3,256,256]{3,2,1,0:T(8,128)(2,1)}) fusion(bf16[2,3,3,256,256]{4,3,2,1,0:T(8,128)(2,1)} %param.14), kind=kLoop, calls=%fused_computation.46 | loop fusion | bytes 4718592 | tf_op jit(solution)/shard_map/squeeze | solution.py:93
  54.1 2.8 %all-to-all-done.2 = bf16[8,128,32]{1,2,0:T(8,128)(2,1)S(1)} async-done(((bf16[8,128,32]{1,2,0:T(8,128)(2,1)}), bf16[8,128,32]{1,2,0:T(8,128)(2,1)S(1)}, u32[]{:S(2)}, u32[]{:S(2)}) %all-to-all-start.2) | async-done | bytes 65568 | tf_op jit(solution)/shard_map/all_to_all | solution.py:75
  56.9 1.1 reshape.236
  58.0 1.2 copy.43
  59.3 6.2 %collective-permute-start.2 = (bf16[4,1,32,256]{3,2,1,0:T(8,128)(2,1)S(1)}, bf16[4,1,32,256]{3,2,1,0:T(8,128)(2,1)S(1)}, u32[]{:S(2)}, u32[]{:S(2)}) collective-permute-start(bf16[4,1,32,256]{3,2,1,0:T(8,128)(2,1)S(1)} %get-tuple-element.159), channel_id=1, source_target_pairs={{0,1},{1,2},{2,3},{4,5},{5,6},{6,7},{8,9},{9,10},{10,11},{12,13},{... | collective-permute-start | bytes 196616 | tf_op jit(solution)/shard_map/ppermute | solution.py:24
  65.6 1.9 %collective-permute-start.3 = (bf16[4,1,32,256]{3,2,1,0:T(8,128)(2,1)S(1)}, bf16[4,1,32,256]{3,2,1,0:T(8,128)(2,1)S(1)}, u32[]{:S(2)}, u32[]{:S(2)}) collective-permute-start(bf16[4,1,32,256]{3,2,1,0:T(8,128)(2,1)S(1)} %get-tuple-element.160), channel_id=1, source_target_pairs={{1,0},{2,1},{3,2},{5,4},{6,5},{7,6},{9,8},{10,9},{11,10},{13,12},{... | collective-permute-start | bytes 196616 | tf_op jit(solution)/shard_map/ppermute | solution.py:26
  67.6 3.6 %collective-permute-done.3 = bf16[4,1,32,256]{3,2,1,0:T(8,128)(2,1)S(1)} collective-permute-done((bf16[4,1,32,256]{3,2,1,0:T(8,128)(2,1)S(1)}, bf16[4,1,32,256]{3,2,1,0:T(8,128)(2,1)S(1)}, u32[]{:S(2)}, u32[]{:S(2)}) %collective-permute-start.3) | collective-permute-done | bytes 65568 | tf_op jit(solution)/shard_map/ppermute | solution.py:26
  71.4 0.3 fusion.43
  71.7 1.0 copy-done.1
  74.5 0.2 fusion.4
  75.0 1.9 %collective-permute-start.4 = (bf16[4,1,32,256]{3,2,1,0:T(8,128)(2,1)S(1)}, bf16[4,1,32,256]{3,2,1,0:T(8,128)(2,1)S(1)}, u32[]{:S(2)}, u32[]{:S(2)}) collective-permute-start(bf16[4,1,32,256]{3,2,1,0:T(8,128)(2,1)S(1)} %get-tuple-element.155), channel_id=1, source_target_pairs={{0,1},{1,2},{2,3},{4,5},{5,6},{6,7},{8,9},{9,10},{10,11},{12,13},{... | collective-permute-start | bytes 196616 | tf_op jit(solution)/shard_map/ppermute | solution.py:24
  77.0 2.4 %collective-permute-start.5 = (bf16[4,1,32,256]{3,2,1,0:T(8,128)(2,1)S(1)}, bf16[4,1,32,256]{3,2,1,0:T(8,128)(2,1)S(1)}, u32[]{:S(2)}, u32[]{:S(2)}) collective-permute-start(bf16[4,1,32,256]{3,2,1,0:T(8,128)(2,1)S(1)} %get-tuple-element.156), channel_id=1, source_target_pairs={{1,0},{2,1},{3,2},{5,4},{6,5},{7,6},{9,8},{10,9},{11,10},{13,12},{... | collective-permute-start | bytes 196616 | tf_op jit(solution)/shard_map/ppermute | solution.py:26
  79.4 0.8 copy.41
  80.2 3.4 %all-to-all-start.4 = ((f32[1,1,256]{1,0,2:T(1,128)}), f32[1,1,256]{1,0,2:T(1,128)S(1)}, u32[]{:S(2)}, u32[]{:S(2)}) async-start(f32[1,1,256]{1,0,2:T(1,128)} %copy.41), calls=%async_computation.4 | async-start | bytes 262144 | tf_op jit(solution)/shard_map/all_to_all | solution.py:70
  83.6 7.0 %all-to-all-done.4 = f32[1,1,256]{1,0,2:T(1,128)S(1)} async-done(((f32[1,1,256]{1,0,2:T(1,128)}), f32[1,1,256]{1,0,2:T(1,128)S(1)}, u32[]{:S(2)}, u32[]{:S(2)}) %all-to-all-start.4) | async-done | bytes 1056 | tf_op jit(solution)/shard_map/all_to_all | solution.py:70
  90.6 1.0 reduce.1
  92.0 0.3 fusion.42
  94.5 0.5 while.27
  95.3 0.6 constant_dynamic-update-slice_fusion.15
  96.4 0.6 constant_dynamic-update-slice_fusion.14
  97.1 0.6 constant_dynamic-update-slice_fusion.13
  97.7 0.6 constant_dynamic-update-slice_fusion.12
  98.3 0.6 constant_dynamic-update-slice_fusion.11
  98.9 0.6 constant_dynamic-update-slice_fusion.10
  99.5 0.6 constant_dynamic-update-slice_fusion.9
  100.1 0.6 constant_dynamic-update-slice_fusion.8
  100.7 3.4 %all-to-all-start.3 = ((f32[8,1,128,32]{2,3,1,0:T(8,128)}), f32[8,1,128,32]{2,3,1,0:T(8,128)S(1)}, u32[]{:S(2)}, u32[]{:S(2)}) async-start(f32[8,1,128,32]{2,3,1,0:T(8,128)} %constant_dynamic-update-slice_fusion.8), calls=%async_computation.3 | async-start | bytes 262144 | tf_op jit(solution)/shard_map/all_to_all | solution.py:12
  104.1 6.1 %all-to-all-done.3 = f32[8,1,128,32]{2,3,1,0:T(8,128)S(1)} async-done(((f32[8,1,128,32]{2,3,1,0:T(8,128)}), f32[8,1,128,32]{2,3,1,0:T(8,128)S(1)}, u32[]{:S(2)}, u32[]{:S(2)}) %all-to-all-start.3) | async-done | bytes 131104 | tf_op jit(solution)/shard_map/all_to_all | solution.py:12
  110.9 8.9 %all_to_all.52 = bf16[8,128,32]{1,2,0:T(8,128)(2,1)S(1)} all-to-all(bf16[8,128,32]{1,2,0:T(8,128)(2,1)S(1)} %concatenate.68), channel_id=1, replica_groups=mesh['tm'=8,'rows'=4] {'tm'}, dimensions={0} | all-to-all | bytes 131072 | tf_op jit(solution)/shard_map/all_to_all | solution.py:75
  119.8 0.3 reshape.237
  120.4 4.9 %collective-permute-start.6 = (bf16[4,1,32,256]{3,2,1,0:T(8,128)(2,1)S(1)}, bf16[4,1,32,256]{3,2,1,0:T(8,128)(2,1)S(1)}, u32[]{:S(2)}, u32[]{:S(2)}) collective-permute-start(bf16[4,1,32,256]{3,2,1,0:T(8,128)(2,1)S(1)} %get-tuple-element.151), channel_id=1, source_target_pairs={{0,1},{1,2},{2,3},{4,5},{5,6},{6,7},{8,9},{9,10},{10,11},{12,13},{... | collective-permute-start | bytes 196616 | tf_op jit(solution)/shard_map/ppermute | solution.py:24
  125.3 1.9 %collective-permute-start.7 = (bf16[4,1,32,256]{3,2,1,0:T(8,128)(2,1)S(1)}, bf16[4,1,32,256]{3,2,1,0:T(8,128)(2,1)S(1)}, u32[]{:S(2)}, u32[]{:S(2)}) collective-permute-start(bf16[4,1,32,256]{3,2,1,0:T(8,128)(2,1)S(1)} %get-tuple-element.152), channel_id=1, source_target_pairs={{1,0},{2,1},{3,2},{5,4},{6,5},{7,6},{9,8},{10,9},{11,10},{13,12},{... | collective-permute-start | bytes 196616 | tf_op jit(solution)/shard_map/ppermute | solution.py:26
  127.3 3.6 %collective-permute-done.7 = bf16[4,1,32,256]{3,2,1,0:T(8,128)(2,1)S(1)} collective-permute-done((bf16[4,1,32,256]{3,2,1,0:T(8,128)(2,1)S(1)}, bf16[4,1,32,256]{3,2,1,0:T(8,128)(2,1)S(1)}, u32[]{:S(2)}, u32[]{:S(2)}) %collective-permute-start.7) | collective-permute-done | bytes 65568 | tf_op jit(solution)/shard_map/ppermute | solution.py:26
  131.1 0.3 fusion.41
  133.6 0.9 fusion.22
  (163 shorter events, 13.0 us)
Async XLA Ops:
  0.9 21.8 %collective-permute-start = (bf16[4,1,32,256]{3,2,1,0:T(8,128)(2,1)S(1)}, bf16[4,1,32,256]{3,2,1,0:T(8,128)(2,1)S(1)}, u32[]{:S(2)}, u32[]{:S(2)}) collective-permute-start(bf16[4,1,32,256]{3,2,1,0:T(8,128)(2,1)S(1)} %get-tuple-element.163), channel_id=1, source_target_pairs={{0,1},{1,2},{2,3},{4,5},{5,6},{6,7},{8,9},{9,10},{10,11},{12,13},{... | collective-permute-start | bytes 196616 | tf_op jit(solution)/shard_map/ppermute | solution.py:24
  5.4 17.2 %collective-permute-start.1 = (bf16[4,1,32,256]{3,2,1,0:T(8,128)(2,1)S(1)}, bf16[4,1,32,256]{3,2,1,0:T(8,128)(2,1)S(1)}, u32[]{:S(2)}, u32[]{:S(2)}) collective-permute-start(bf16[4,1,32,256]{3,2,1,0:T(8,128)(2,1)S(1)} %get-tuple-element.164), channel_id=1, source_target_pairs={{1,0},{2,1},{3,2},{5,4},{6,5},{7,6},{9,8},{10,9},{11,10},{13,12},{... | collective-permute-start | bytes 196616 | tf_op jit(solution)/shard_map/ppermute | solution.py:26
  9.7 11.7 %all-to-all-start.1 = ((f32[1,1,256]{1,0,2:T(1,128)}), f32[1,1,256]{1,0,2:T(1,128)S(1)}, u32[]{:S(2)}, u32[]{:S(2)}) async-start(f32[1,1,256]{1,0,2:T(1,128)} %copy.31), calls=%async_computation.1 | async-start | bytes 262144 | tf_op jit(solution)/shard_map/all_to_all | solution.py:70
  15.2 7.4 %copy-start = (bf16[4,4,32,256]{3,2,1,0:T(8,128)(2,1)S(1)}, bf16[4,4,32,256]{3,2,1,0:T(8,128)(2,1)}, u32[]{:S(2)}) copy-start(bf16[4,4,32,256]{3,2,1,0:T(8,128)(2,1)} %param.10) | copy-start | bytes 786436
  35.9 10.6 %all-to-all-start = ((f32[8,1,128,32]{2,3,1,0:T(8,128)}), f32[8,1,128,32]{2,3,1,0:T(8,128)S(1)}, u32[]{:S(2)}, u32[]{:S(2)}) async-start(f32[8,1,128,32]{2,3,1,0:T(8,128)} %constant_dynamic-update-slice_fusion), calls=%async_computation | async-start | bytes 262144 | tf_op jit(solution)/shard_map/all_to_all | solution.py:12
  47.8 9.1 %all-to-all-start.2 = ((bf16[8,128,32]{1,2,0:T(8,128)(2,1)}), bf16[8,128,32]{1,2,0:T(8,128)(2,1)S(1)}, u32[]{:S(2)}, u32[]{:S(2)}) async-start(bf16[8,128,32]{1,2,0:T(8,128)(2,1)} %concatenate.59), calls=%async_computation.2 | async-start | bytes 131072 | tf_op jit(solution)/shard_map/all_to_all | solution.py:75
  56.9 10.6 %copy-start.2 = (f32[2,256]{1,0:T(2,128)S(1)}, f32[2,256]{1,0:T(2,128)}, u32[]{:S(2)}) copy-start(f32[2,256]{1,0:T(2,128)} %param.15) | copy-start | bytes 6148
  59.3 8.2 %collective-permute-start.2 = (bf16[4,1,32,256]{3,2,1,0:T(8,128)(2,1)S(1)}, bf16[4,1,32,256]{3,2,1,0:T(8,128)(2,1)S(1)}, u32[]{:S(2)}, u32[]{:S(2)}) collective-permute-start(bf16[4,1,32,256]{3,2,1,0:T(8,128)(2,1)S(1)} %get-tuple-element.159), channel_id=1, source_target_pairs={{0,1},{1,2},{2,3},{4,5},{5,6},{6,7},{8,9},{9,10},{10,11},{12,13},{... | collective-permute-start | bytes 196616 | tf_op jit(solution)/shard_map/ppermute | solution.py:24
  65.6 5.6 %collective-permute-start.3 = (bf16[4,1,32,256]{3,2,1,0:T(8,128)(2,1)S(1)}, bf16[4,1,32,256]{3,2,1,0:T(8,128)(2,1)S(1)}, u32[]{:S(2)}, u32[]{:S(2)}) collective-permute-start(bf16[4,1,32,256]{3,2,1,0:T(8,128)(2,1)S(1)} %get-tuple-element.160), channel_id=1, source_target_pairs={{1,0},{2,1},{3,2},{5,4},{6,5},{7,6},{9,8},{10,9},{11,10},{13,12},{... | collective-permute-start | bytes 196616 | tf_op jit(solution)/shard_map/ppermute | solution.py:26
  71.4 1.3 copy-start.1
  75.0 16.8 %collective-permute-start.4 = (bf16[4,1,32,256]{3,2,1,0:T(8,128)(2,1)S(1)}, bf16[4,1,32,256]{3,2,1,0:T(8,128)(2,1)S(1)}, u32[]{:S(2)}, u32[]{:S(2)}) collective-permute-start(bf16[4,1,32,256]{3,2,1,0:T(8,128)(2,1)S(1)} %get-tuple-element.155), channel_id=1, source_target_pairs={{0,1},{1,2},{2,3},{4,5},{5,6},{6,7},{8,9},{9,10},{10,11},{12,13},{... | collective-permute-start | bytes 196616 | tf_op jit(solution)/shard_map/ppermute | solution.py:24
  77.0 14.8 %collective-permute-start.5 = (bf16[4,1,32,256]{3,2,1,0:T(8,128)(2,1)S(1)}, bf16[4,1,32,256]{3,2,1,0:T(8,128)(2,1)S(1)}, u32[]{:S(2)}, u32[]{:S(2)}) collective-permute-start(bf16[4,1,32,256]{3,2,1,0:T(8,128)(2,1)S(1)} %get-tuple-element.156), channel_id=1, source_target_pairs={{1,0},{2,1},{3,2},{5,4},{6,5},{7,6},{9,8},{10,9},{11,10},{13,12},{... | collective-permute-start | bytes 196616 | tf_op jit(solution)/shard_map/ppermute | solution.py:26
  80.2 10.4 %all-to-all-start.4 = ((f32[1,1,256]{1,0,2:T(1,128)}), f32[1,1,256]{1,0,2:T(1,128)S(1)}, u32[]{:S(2)}, u32[]{:S(2)}) async-start(f32[1,1,256]{1,0,2:T(1,128)} %copy.41), calls=%async_computation.4 | async-start | bytes 262144 | tf_op jit(solution)/shard_map/all_to_all | solution.py:70
  100.7 9.5 %all-to-all-start.3 = ((f32[8,1,128,32]{2,3,1,0:T(8,128)}), f32[8,1,128,32]{2,3,1,0:T(8,128)S(1)}, u32[]{:S(2)}, u32[]{:S(2)}) async-start(f32[8,1,128,32]{2,3,1,0:T(8,128)} %constant_dynamic-update-slice_fusion.8), calls=%async_computation.3 | async-start | bytes 262144 | tf_op jit(solution)/shard_map/all_to_all | solution.py:12
  120.4 6.9 %collective-permute-start.6 = (bf16[4,1,32,256]{3,2,1,0:T(8,128)(2,1)S(1)}, bf16[4,1,32,256]{3,2,1,0:T(8,128)(2,1)S(1)}, u32[]{:S(2)}, u32[]{:S(2)}) collective-permute-start(bf16[4,1,32,256]{3,2,1,0:T(8,128)(2,1)S(1)} %get-tuple-element.151), channel_id=1, source_target_pairs={{0,1},{1,2},{2,3},{4,5},{5,6},{6,7},{8,9},{9,10},{10,11},{12,13},{... | collective-permute-start | bytes 196616 | tf_op jit(solution)/shard_map/ppermute | solution.py:24
  125.3 5.6 %collective-permute-start.7 = (bf16[4,1,32,256]{3,2,1,0:T(8,128)(2,1)S(1)}, bf16[4,1,32,256]{3,2,1,0:T(8,128)(2,1)S(1)}, u32[]{:S(2)}, u32[]{:S(2)}) collective-permute-start(bf16[4,1,32,256]{3,2,1,0:T(8,128)(2,1)S(1)} %get-tuple-element.152), channel_id=1, source_target_pairs={{1,0},{2,1},{3,2},{5,4},{6,5},{7,6},{9,8},{10,9},{11,10},{13,12},{... | collective-permute-start | bytes 196616 | tf_op jit(solution)/shard_map/ppermute | solution.py:26
